TPU v7x, 128 devices: a whole 4x4x4 slice. The times are simulated.
128 devices in a mesh: sec: 2 (over y_hi), dev: 32 (over z, x, core), tp: 2 (over y_lo).
Axes of the slice: x: 4, y: 4 (y_hi: 2, y_lo: 2; y = y_hi * 2 + y_lo), z: 4, core: 2. Of those that a mesh axis runs over, the one named last changes fastest.
Arguments:
- queries: bfloat16 [512, 8192], P(('sec', 'dev'), 'tp'), may hold values from -6 to 6
- new_keys: bfloat16 [512, 1024], P(('sec', 'dev'), 'tp'), may hold values from -6 to 6
- token_values: bfloat16 [512, 1024], P(('sec', 'dev'), 'tp'), may hold values from -6 to 6
- key_cache: bfloat16 [512, 256, 1024], P(('sec', 'dev'), None, 'tp'), may hold values from -6 to 6
- stored_values: bfloat16 [512, 256, 1024], P(('sec', 'dev'), None, 'tp'), may hold values from -6 to 6
- cache_lengths: int32 [512], P(('sec', 'dev')), may hold values from 1 to 256, 65536 in all
- residual: bfloat16 [512, 8192], P(('sec', 'dev', 'tp')), may hold values from -6 to 6
- norm_gain: float32 [8192], replicated, may hold values from 0.25 to 1.75
- active: int32 [512, 16], P(('sec', 'dev', 'tp')), may hold values from 0 to 127, all different within a row; in each aligned block of 4 rows (0 to 3, 4 to 7, ...) at most 3 rows name the same one
- gate_weight: bfloat16 [8192, 16384], P(None, ('sec', 'dev', 'tp')), may hold values from -0.0625 to 0.0625
- up_weight: bfloat16 [8192, 16384], P(None, ('sec', 'dev', 'tp')), may hold values from -0.0625 to 0.0625
- down_weight: bfloat16 [16384, 8192], P(('sec', 'dev', 'tp')), may hold values from -0.125 to 0.125
Outputs:
- layer_out: bfloat16 [512, 8192], P(('sec', 'dev', 'tp'))
Inputs may be any that keep to these rules, and one draw needn't show every extreme that they name: `cache_lengths`: the largest length is 256 in every draw. `active`: the bundles of one row are distinct. Among the 4 rows of one device (aligned blocks of rows), no bundle is named by more than 3 rows, and some bundle reaches 3.
All inputs are finite; a program needn't handle non-finite values. No bound on the sum of `cache_lengths` on one device may be relied on, other than what follows from the above.
Results may differ from a plain program's by a relative error of at most 0.007.
Values may be sent and summed in bfloat16 or wider, within the bound.
A program may use at most 128 MiB of HBM per device.

v0:
```python
import jax
import jax.numpy as jnp
from jax import lax
from jax.sharding import PartitionSpec as P

HEAD_SIZE = 128
CACHE_POSITIONS = 256
epsilon = 1e-05


def attend(queries, new_keys, token_values, key_cache, stored_values, cache_lengths):
    request_count, query_width = queries.shape
    kv_width = new_keys.shape[1]
    kv_heads = kv_width // HEAD_SIZE
    group_width = query_width // kv_width
    scaling = HEAD_SIZE ** (-0.5)
    grouped = queries.reshape(request_count, kv_heads, group_width, HEAD_SIZE)
    cached_keys = key_cache.reshape(request_count, CACHE_POSITIONS, kv_heads, HEAD_SIZE)
    cached_values = stored_values.reshape(request_count, CACHE_POSITIONS, kv_heads, HEAD_SIZE)
    scores = (
        jnp.einsum("rkgd,rckd->rkgc", grouped, cached_keys, preferred_element_type=jnp.float32)
        * scaling
    )
    visible = jnp.arange(CACHE_POSITIONS, dtype=jnp.int32)[None, :] < cache_lengths[:, None]
    scores = jnp.where(visible[:, None, None, :], scores, -jnp.inf)
    fresh_keys = new_keys.reshape(request_count, kv_heads, HEAD_SIZE)
    fresh_score = (
        jnp.einsum("rkgd,rkd->rkg", grouped, fresh_keys, preferred_element_type=jnp.float32)
        * scaling
    )
    highest = jnp.maximum(jnp.max(scores, axis=-1), fresh_score)
    weights_cache = jnp.exp(scores - highest[..., None])
    weight_fresh = jnp.exp(fresh_score - highest)
    denominator = jnp.sum(weights_cache, axis=-1) + weight_fresh
    probs_cache = (weights_cache / denominator[..., None]).astype(jnp.bfloat16)
    prob_fresh = (weight_fresh / denominator).astype(jnp.bfloat16)
    blended = jnp.einsum(
        "rkgc,rckd->rkgd", probs_cache, cached_values, preferred_element_type=jnp.float32
    )
    fresh_values = token_values.reshape(request_count, kv_heads, 1, HEAD_SIZE).astype(jnp.float32)
    blended = blended + prob_fresh[..., None].astype(jnp.float32) * fresh_values
    return blended.reshape(request_count, query_width).astype(jnp.bfloat16)


def feed_forward(row_block, gate_weight, up_weight, selected):
    gate_value = jnp.dot(row_block, gate_weight, preferred_element_type=jnp.float32)
    up_value = jnp.dot(row_block, up_weight, preferred_element_type=jnp.float32)
    return (jax.nn.relu(gate_value) * up_value * selected).astype(jnp.bfloat16)


def shards(
    queries,
    new_keys,
    token_values,
    key_cache,
    stored_values,
    cache_lengths,
    residual,
    norm_gain,
    active,
    gate_weight,
    up_weight,
    down_weight,
):
    context = attend(queries, new_keys, token_values, key_cache, stored_values, cache_lengths)
    context = lax.all_to_all(context, "tp", split_axis=0, concat_axis=1, tiled=True)
    stream = residual.astype(jnp.float32) + context.astype(jnp.float32)
    mean_square = jnp.mean(stream * stream, axis=1, keepdims=True)
    normed = (stream * lax.rsqrt(mean_square + epsilon) * norm_gain[None, :]).astype(jnp.bfloat16)
    local_rows, model_width = normed.shape
    device_count = lax.axis_size(("sec", "dev", "tp"))
    top_count = active.shape[1]
    slot_limit = max(3, (2 * local_rows * top_count + device_count - 1) // device_count)
    targets = jnp.arange(device_count, dtype=jnp.int32)
    naming = jnp.any(active[:, :, None] == targets[None, None, :], axis=1).astype(jnp.int32)
    earlier = jnp.cumsum(naming, axis=0) - naming
    slot_ids = jnp.arange(slot_limit, dtype=jnp.int32)
    placed = (
        (naming.T[:, None, :] == 1) & (earlier.T[:, None, :] == slot_ids[None, :, None])
    ).astype(jnp.bfloat16)
    outgoing = jnp.einsum("bsr,rd->bsd", placed, normed, preferred_element_type=jnp.float32).astype(
        jnp.bfloat16
    )
    received = lax.all_to_all(
        outgoing, ("sec", "dev", "tp"), split_axis=0, concat_axis=0, tiled=True
    )
    slot_count = received.shape[1]
    flat_rows = received.reshape(device_count * slot_count, model_width)
    hidden = feed_forward(flat_rows, gate_weight, up_weight, 1.0)
    partial_terms = jnp.dot(hidden, down_weight, preferred_element_type=jnp.float32)
    partial_terms = partial_terms.reshape(device_count, slot_count, model_width)
    returned = lax.all_to_all(
        partial_terms.astype(jnp.bfloat16),
        ("sec", "dev", "tp"),
        split_axis=0,
        concat_axis=0,
        tiled=True,
    ).astype(partial_terms.dtype)
    update = jnp.einsum(
        "bsr,bsd->rd", placed.astype(jnp.float32), returned, precision=lax.Precision.HIGHEST
    )
    return (stream + update).astype(jnp.bfloat16)


def solution(mesh):
    return jax.shard_map(
        shards,
        mesh=mesh,
        in_specs=(
            P(("sec", "dev"), "tp"),
            P(("sec", "dev"), "tp"),
            P(("sec", "dev"), "tp"),
            P(("sec", "dev"), None, "tp"),
            P(("sec", "dev"), None, "tp"),
            P(("sec", "dev")),
            P(("sec", "dev", "tp"), None),
            P(),
            P(("sec", "dev", "tp"), None),
            P(None, ("sec", "dev", "tp")),
            P(None, ("sec", "dev", "tp")),
            P(("sec", "dev", "tp"), None),
        ),
        out_specs=P(("sec", "dev", "tp"), None),
        check_vma=False,
    )
```

profile of v0, /device:TPU:2, one launch (start us, length us, event | category | flops | bytes accessed | tf_op | source)
XLA Modules:
  0.0 301.2 jit_solution(82121312440829299)
XLA Ops:
  0.0 0.0 copy-start
  0.0 0.0 copy-start.4
  0.0 0.9 iota_compare_fusion.1
  0.9 0.8 bitcast_convert_fusion
  1.7 1.0 fusion.29
  2.7 2.4 fusion.43
  5.1 0.0 copy-start.3
  5.1 0.2 fusion.22
  5.3 0.0 copy-start.1
  5.4 0.0 copy-done.4
  5.4 0.0 copy-start.2
  5.4 0.5 fusion.19
  5.8 0.7 convert_element_type.74
  6.5 3.3 %all-to-all-start = ((bf16[2,4,4096]{2,1,0:T(4,128)(2,1)}), bf16[2,4,4096]{2,1,0:T(4,128)(2,1)S(1)}, u32[]{:S(2)}, u32[]{:S(2)}) async-start(bf16[2,4,4096]{2,1,0:T(4,128)(2,1)} %convert_element_type.74), calls=%async_computation | async-start | bytes 131072 | tf_op jit(solution)/shard_map/all_to_all | solution.py:66
  9.8 0.0 copy-done.3
  9.8 0.1 fusion.32
  10.0 3.9 %all-to-all-done = bf16[2,4,4096]{2,1,0:T(4,128)(2,1)S(1)} async-done(((bf16[2,4,4096]{2,1,0:T(4,128)(2,1)}), bf16[2,4,4096]{2,1,0:T(4,128)(2,1)S(1)}, u32[]{:S(2)}, u32[]{:S(2)}) %all-to-all-start) | async-done | bytes 65568 | tf_op jit(solution)/shard_map/all_to_all | solution.py:66
  13.9 0.0 copy-done.1
  13.9 0.2 multiply_reduce_fusion
  14.1 0.0 copy-done.2
  14.1 4.6 %convolution_convert_fusion.1 = bf16[128,3,8192]{2,0,1:T(8,128)(2,1)} fusion(f32[8192]{0:T(1024)S(1)} %copy-done.2, f32[4]{0:T(128)S(1)} %add_rsqrt_fusion, f32[4,8192]{1,0:T(4,128)S(1)} %bitcast.57, bf16[4,8192]{1,0:T(4,128)(2,1)S(1)} %copy-done.1, s32[128,4]{0,1:T(4,128)S(1)} %subtract_bitcast_fusion, pred[128,4]{0,1:T(4,128)(4,1)S(1)} %get-tuple-element.7), kind=kOutput, calls=%fused_computation.1 | convolution fusion | flops 28478464 | bytes 6523408 | tf_op jit(solution)/shard_map/bsr,rd->bsd/dot_general | solution.py:81
  18.7 11.4 %copy.34 = bf16[128,3,8192]{2,1,0:T(4,128)(2,1)} copy(bf16[128,3,8192]{2,0,1:T(8,128)(2,1)} %convolution_convert_fusion.1) | data formatting | bytes 12582912 | tf_op jit(solution)/shard_map/convert_element_type | solution.py:81
  30.1 112.5 %all_to_all.20 = bf16[128,3,8192]{2,1,0:T(4,128)(2,1)} all-to-all(bf16[128,3,8192]{2,1,0:T(4,128)(2,1)} %copy.34), channel_id=1, replica_groups=mesh['sec'=2,'dev'=32,'tp'=2] {'sec','dev','tp'}, dimensions={0} | all-to-all | bytes 12582912 | tf_op jit(solution)/shard_map/all_to_all | solution.py:84
  142.6 13.7 %reshape.73 = bf16[384,8192]{1,0:T(8,128)(2,1)} reshape(bf16[128,3,8192]{2,1,0:T(4,128)(2,1)} %all_to_all.20) | data formatting | bytes 12582912 | tf_op jit(solution)/shard_map/reshape | solution.py:88
  156.3 5.2 %convolution_maximum_fusion = f32[384,128]{1,0:T(8,128)S(1)} fusion(bf16[384,8192]{1,0:T(8,128)(2,1)} %reshape.73, bf16[8192,128]{1,0:T(8,128)(2,1)} %param.21), kind=kOutput, calls=%fused_computation.15 | convolution fusion | flops 805355520 | bytes 8585216 | tf_op jit(solution)/shard_map/dot_general | solution.py:46
  161.5 0.0 copy-done
  161.5 12.8 %convolution_convert_fusion = bf16[384,8192]{1,0:T(8,128)(2,1)} fusion(bf16[128,8192]{1,0:T(8,128)(2,1)S(1)} %copy-done, f32[384,128]{1,0:T(8,128)S(1)} %convolution_maximum_fusion, bf16[384,8192]{1,0:T(8,128)(2,1)} %reshape.73, bf16[8192,128]{1,0:T(8,128)(2,1)} %param.22), kind=kOutput, calls=%fused_computation | convolution fusion | flops 1613856768 | bytes 16973824 | tf_op jit(solution)/shard_map/dot_general | solution.py:90
  174.3 12.8 %convert_element_type.83 = bf16[128,3,8192]{2,1,0:T(4,128)(2,1)} reshape(bf16[384,8192]{1,0:T(8,128)(2,1)} %convolution_convert_fusion) | data formatting | bytes 12582912 | tf_op jit(solution)/shard_map/convert_element_type | solution.py:93
  187.1 106.7 %all_to_all.21 = bf16[128,3,8192]{2,1,0:T(4,128)(2,1)S(1)} all-to-all(bf16[128,3,8192]{2,1,0:T(4,128)(2,1)} %convert_element_type.83), channel_id=1, replica_groups=mesh['sec'=2,'dev'=32,'tp'=2] {'sec','dev','tp'}, dimensions={0} | all-to-all | bytes 12582912 | tf_op jit(solution)/shard_map/all_to_all | solution.py:92
  293.9 7.3 %fusion.1 = bf16[4,8192]{1,0:T(4,128)(2,1)} fusion(bf16[128,3,8192]{2,1,0:T(4,128)(2,1)S(1)} %all_to_all.21, f32[4,8192]{1,0:T(4,128)S(1)} %bitcast.58, bf16[4,8192]{1,0:T(4,128)(2,1)S(1)} %copy-done.1, s32[128,4]{0,1:T(4,128)S(1)} %subtract_bitcast_fusion, pred[128,4]{0,1:T(4,128)(4,1)S(1)} %get-tuple-element.7), kind=kOutput, calls=%fused_computation.4 | convolution fusion | flops 25299968 | bytes 6556160 | tf_op jit(solution)/shard_map/bsr,bsd->rd/dot_general | solution.py:99
  (8 shorter events, 0.1 us)
Async XLA Ops:
  0.0 161.5 %copy-start = (bf16[128,8192]{1,0:T(8,128)(2,1)S(1)}, bf16[128,8192]{1,0:T(8,128)(2,1)}, u32[]{:S(2)}) copy-start(bf16[128,8192]{1,0:T(8,128)(2,1)} %param.23) | copy-start | bytes 6291460
  0.0 5.4 %copy-start.4 = (bf16[8,256,512]{2,1,0:T(8,128)(2,1)S(1)}, bf16[8,256,512]{2,1,0:T(8,128)(2,1)}, u32[]{:S(2)}) copy-start(bf16[8,256,512]{2,1,0:T(8,128)(2,1)} %param.16) | copy-start | bytes 6291460
  5.1 4.7 %copy-start.3 = (s32[4,16]{1,0:T(4,128)S(1)}, s32[4,16]{1,0:T(4,128)}, u32[]{:S(2)}) copy-start(s32[4,16]{1,0:T(4,128)} %param.20) | copy-start | bytes 772
  5.3 8.6 %copy-start.1 = (bf16[4,8192]{1,0:T(4,128)(2,1)S(1)}, bf16[4,8192]{1,0:T(4,128)(2,1)}, u32[]{:S(2)}) copy-start(bf16[4,8192]{1,0:T(4,128)(2,1)} %param.18) | copy-start | bytes 196612
  5.4 8.8 %copy-start.2 = (f32[8192]{0:T(1024)S(1)}, f32[8192]{0:T(1024)}, u32[]{:S(2)}) copy-start(f32[8192]{0:T(1024)} %param.19) | copy-start | bytes 98308
  6.5 7.4 %all-to-all-start = ((bf16[2,4,4096]{2,1,0:T(4,128)(2,1)}), bf16[2,4,4096]{2,1,0:T(4,128)(2,1)S(1)}, u32[]{:S(2)}, u32[]{:S(2)}) async-start(bf16[2,4,4096]{2,1,0:T(4,128)(2,1)} %convert_element_type.74), calls=%async_computation | async-start | bytes 131072 | tf_op jit(solution)/shard_map/all_to_all | solution.py:66
where the time goes:
time: 302 us; the launch traced here: 301 us
  blocking collectives  219 us (73%)
  local copies, waits for them, and re-layouts  38.6 us (13%)
  matrix products  33.7 us (11%)
  waiting for transfers between devices  3.94 us (1%)
  starting transfers between devices  3.3 us (1%)
    all_to_all x1, blocking collectives, shards(): lax.all_to_all(outgoing, ('sec', 'dev', 'tp'), split_axis=0, concat_axis=...  113 us
    all_to_all x1, blocking collectives, shards(): lax.all_to_all(partial_terms.astype(jnp.bfloat16), ('sec', 'dev', 'tp'),...  107 us
    reshape x1, local copies, waits for them, and re-layouts, shards(): flat_rows = received.reshape(device_count * slot_count, model_width)  13.7 us
    convert_element_type x1, local copies, waits for them, and re-layouts, shards(): partial_terms.astype(jnp.bfloat16)  12.8 us
    dot_general x1, matrix products, shards(): jnp.dot(hidden, down_weight, preferred_element_type=jnp.float32)  12.8 us
    convert_element_type x1, local copies, waits for them, and re-layouts, shards(): jnp.einsum('bsr,rd->bsd', placed, normed, preferred_element_type=jnp.floa...  11.4 us
    dot_general x1, matrix products, shards(): jnp.einsum('bsr,bsd->rd', placed.astype(jnp.float32), returned, precision...  7.3 us
  transfers between devices with their start and end apart: 1, of which 1 were waited for; matrix products, arithmetic and copies ran while one was open for 0% of the time, Pallas kernels for 0%

commit v1 on v0

--- a/solution.py
+++ b/solution.py
@@ -63,7 +63,10 @@
     down_weight,
 ):
     context = attend(queries, new_keys, token_values, key_cache, stored_values, cache_lengths)
-    context = lax.all_to_all(context, "tp", split_axis=0, concat_axis=1, tiled=True)
+    context = jnp.concatenate(
+        lax.all_to_all(jnp.stack(jnp.split(context, lax.axis_size("tp"), axis=0)), "tp", 0, 0),
+        axis=1,
+    )
     stream = residual.astype(jnp.float32) + context.astype(jnp.float32)
     mean_square = jnp.mean(stream * stream, axis=1, keepdims=True)
     normed = (stream * lax.rsqrt(mean_square + epsilon) * norm_gain[None, :]).astype(jnp.bfloat16)

time: 302 us -> 302 us (level)
  no operation moved by 1% of the time
where the time goes in v1:
time: 302 us; the launch traced here: 301 us
  blocking collectives  219 us (73%)
  local copies, waits for them, and re-layouts  38 us (13%)
  matrix products  33.7 us (11%)
  waiting for transfers between devices  3.94 us (1%)
  starting transfers between devices  3.3 us (1%)
    all_to_all x1, blocking collectives, shards(): lax.all_to_all(outgoing, ('sec', 'dev', 'tp'), split_axis=0, concat_axis=...  113 us
    all_to_all x1, blocking collectives, shards(): lax.all_to_all(partial_terms.astype(jnp.bfloat16), ('sec', 'dev', 'tp'),...  107 us
    reshape x1, local copies, waits for them, and re-layouts, shards(): flat_rows = received.reshape(device_count * slot_count, model_width)  13.7 us
    convert_element_type x1, local copies, waits for them, and re-layouts, shards(): partial_terms.astype(jnp.bfloat16)  12.8 us
    dot_general x1, matrix products, shards(): jnp.dot(hidden, down_weight, preferred_element_type=jnp.float32)  12.8 us
    convert_element_type x1, local copies, waits for them, and re-layouts, shards(): jnp.einsum('bsr,rd->bsd', placed, normed, preferred_element_type=jnp.floa...  11.4 us
    dot_general x1, matrix products, shards(): jnp.einsum('bsr,bsd->rd', placed.astype(jnp.float32), returned, precision...  7.3 us
  transfers between devices with their start and end apart: 1, of which 1 were waited for; matrix products, arithmetic and copies ran while one was open for 0% of the time, Pallas kernels for 0%

profile of v1, /device:TPU:2, one launch (start us, length us, event | category | flops | bytes accessed | tf_op | source)
XLA Modules:
  0.0 301.2 jit_solution(1741247206189230547)
XLA Ops:
  0.0 0.0 copy-start
  0.0 0.0 copy-start.4
  0.0 0.9 iota_compare_fusion.1
  0.9 0.8 bitcast_convert_fusion
  1.7 1.0 fusion.29
  2.7 2.4 fusion.44
  5.1 0.2 fusion.22
  5.3 0.0 copy-start.3
  5.4 0.0 copy-done.4
  5.4 0.0 copy-start.1
  5.4 0.0 copy-start.2
  5.4 0.5 fusion.19
  5.9 0.7 pad_maximum_fusion
  6.6 3.3 %all-to-all-start = ((bf16[2,4,4096]{2,1,0:T(4,128)(2,1)}), bf16[2,4,4096]{2,1,0:T(4,128)(2,1)S(1)}, u32[]{:S(2)}, u32[]{:S(2)}) async-start(bf16[2,4,4096]{2,1,0:T(4,128)(2,1)} %pad_maximum_fusion), calls=%async_computation | async-start | bytes 131072 | tf_op jit(solution)/shard_map/all_to_all | solution.py:67
  9.9 0.0 copy-done.3
  9.9 0.1 fusion.32
  10.0 3.9 %all-to-all-done = bf16[2,4,4096]{2,1,0:T(4,128)(2,1)S(1)} async-done(((bf16[2,4,4096]{2,1,0:T(4,128)(2,1)}), bf16[2,4,4096]{2,1,0:T(4,128)(2,1)S(1)}, u32[]{:S(2)}, u32[]{:S(2)}) %all-to-all-start) | async-done | bytes 65568 | tf_op jit(solution)/shard_map/all_to_all | solution.py:67
  14.0 0.0 copy-done.1
  14.0 0.2 multiply_reduce_fusion
  14.2 0.0 copy-done.2
  14.2 4.6 %convolution_convert_fusion.1 = bf16[128,3,8192]{2,0,1:T(8,128)(2,1)} fusion(f32[8192]{0:T(1024)S(1)} %copy-done.2, f32[4]{0:T(128)S(1)} %add_rsqrt_fusion, f32[4,8192]{1,0:T(4,128)S(1)} %bitcast.59, bf16[4,8192]{1,0:T(4,128)(2,1)S(1)} %copy-done.1, s32[128,4]{0,1:T(4,128)S(1)} %subtract_bitcast_fusion, pred[128,4]{0,1:T(4,128)(4,1)S(1)} %get-tuple-element.9), kind=kOutput, calls=%fused_computation.1 | convolution fusion | flops 28478464 | bytes 6523408 | tf_op jit(solution)/shard_map/bsr,rd->bsd/dot_general | solution.py:84
  18.8 11.4 %copy.34 = bf16[128,3,8192]{2,1,0:T(4,128)(2,1)} copy(bf16[128,3,8192]{2,0,1:T(8,128)(2,1)} %convolution_convert_fusion.1) | data formatting | bytes 12582912 | tf_op jit(solution)/shard_map/convert_element_type | solution.py:84
  30.2 112.5 %all_to_all.15 = bf16[128,3,8192]{2,1,0:T(4,128)(2,1)} all-to-all(bf16[128,3,8192]{2,1,0:T(4,128)(2,1)} %copy.34), channel_id=1, replica_groups=mesh['sec'=2,'dev'=32,'tp'=2] {'sec','dev','tp'}, dimensions={0} | all-to-all | bytes 12582912 | tf_op jit(solution)/shard_map/all_to_all | solution.py:87
  142.7 13.7 %reshape.75 = bf16[384,8192]{1,0:T(8,128)(2,1)} reshape(bf16[128,3,8192]{2,1,0:T(4,128)(2,1)} %all_to_all.15) | data formatting | bytes 12582912 | tf_op jit(solution)/shard_map/reshape | solution.py:91
  156.4 5.2 %convolution_maximum_fusion = f32[384,128]{1,0:T(8,128)S(1)} fusion(bf16[384,8192]{1,0:T(8,128)(2,1)} %reshape.75, bf16[8192,128]{1,0:T(8,128)(2,1)} %param.21), kind=kOutput, calls=%fused_computation.15 | convolution fusion | flops 805355520 | bytes 8585216 | tf_op jit(solution)/shard_map/dot_general | solution.py:46
  161.6 0.0 copy-done
  161.6 12.8 %convolution_convert_fusion = bf16[384,8192]{1,0:T(8,128)(2,1)} fusion(bf16[128,8192]{1,0:T(8,128)(2,1)S(1)} %copy-done, f32[384,128]{1,0:T(8,128)S(1)} %convolution_maximum_fusion, bf16[384,8192]{1,0:T(8,128)(2,1)} %reshape.75, bf16[8192,128]{1,0:T(8,128)(2,1)} %param.22), kind=kOutput, calls=%fused_computation | convolution fusion | flops 1613856768 | bytes 16973824 | tf_op jit(solution)/shard_map/dot_general | solution.py:93
  174.4 12.8 %convert_element_type.79 = bf16[128,3,8192]{2,1,0:T(4,128)(2,1)} reshape(bf16[384,8192]{1,0:T(8,128)(2,1)} %convolution_convert_fusion) | data formatting | bytes 12582912 | tf_op jit(solution)/shard_map/convert_element_type | solution.py:96
  187.2 106.7 %all_to_all.16 = bf16[128,3,8192]{2,1,0:T(4,128)(2,1)S(1)} all-to-all(bf16[128,3,8192]{2,1,0:T(4,128)(2,1)} %convert_element_type.79), channel_id=1, replica_groups=mesh['sec'=2,'dev'=32,'tp'=2] {'sec','dev','tp'}, dimensions={0} | all-to-all | bytes 12582912 | tf_op jit(solution)/shard_map/all_to_all | solution.py:95
  293.9 7.3 %fusion.1 = bf16[4,8192]{1,0:T(4,128)(2,1)} fusion(bf16[128,3,8192]{2,1,0:T(4,128)(2,1)S(1)} %all_to_all.16, f32[4,8192]{1,0:T(4,128)S(1)} %bitcast.60, bf16[4,8192]{1,0:T(4,128)(2,1)S(1)} %copy-done.1, s32[128,4]{0,1:T(4,128)S(1)} %subtract_bitcast_fusion, pred[128,4]{0,1:T(4,128)(4,1)S(1)} %get-tuple-element.9), kind=kOutput, calls=%fused_computation.4 | convolution fusion | flops 25299968 | bytes 6556160 | tf_op jit(solution)/shard_map/bsr,bsd->rd/dot_general | solution.py:102
  (11 shorter events, 0.2 us)
Async XLA Ops:
  0.0 161.6 %copy-start = (bf16[128,8192]{1,0:T(8,128)(2,1)S(1)}, bf16[128,8192]{1,0:T(8,128)(2,1)}, u32[]{:S(2)}) copy-start(bf16[128,8192]{1,0:T(8,128)(2,1)} %param.23) | copy-start | bytes 6291460
  0.0 5.3 %copy-start.4 = (bf16[8,256,512]{2,1,0:T(8,128)(2,1)S(1)}, bf16[8,256,512]{2,1,0:T(8,128)(2,1)}, u32[]{:S(2)}) copy-start(bf16[8,256,512]{2,1,0:T(8,128)(2,1)} %param.16) | copy-start | bytes 6291460
  5.3 4.6 %copy-start.3 = (s32[4,16]{1,0:T(4,128)S(1)}, s32[4,16]{1,0:T(4,128)}, u32[]{:S(2)}) copy-start(s32[4,16]{1,0:T(4,128)} %param.20) | copy-start | bytes 772
  5.4 8.6 %copy-start.1 = (bf16[4,8192]{1,0:T(4,128)(2,1)S(1)}, bf16[4,8192]{1,0:T(4,128)(2,1)}, u32[]{:S(2)}) copy-start(bf16[4,8192]{1,0:T(4,128)(2,1)} %param.18) | copy-start | bytes 196612
  5.4 8.8 %copy-start.2 = (f32[8192]{0:T(1024)S(1)}, f32[8192]{0:T(1024)}, u32[]{:S(2)}) copy-start(f32[8192]{0:T(1024)} %param.19) | copy-start | bytes 98308
  6.6 7.4 %all-to-all-start = ((bf16[2,4,4096]{2,1,0:T(4,128)(2,1)}), bf16[2,4,4096]{2,1,0:T(4,128)(2,1)S(1)}, u32[]{:S(2)}, u32[]{:S(2)}) async-start(bf16[2,4,4096]{2,1,0:T(4,128)(2,1)} %pad_maximum_fusion), calls=%async_computation | async-start | bytes 131072 | tf_op jit(solution)/shard_map/all_to_all | solution.py:67
